TPU v7x, 512 devices: a whole 4x4x16 slice. The times are simulated.
512 devices in a mesh: row: 16 (over y, x), col: 32 (over z, core).
Axes of the slice: x: 4, y: 4, z: 16, core: 2. Of those that a mesh axis runs over, the one named last changes fastest.
Arguments:
- out_grad: bfloat16 [2048, 8192], P('col', 'row'), may hold values from -6 to 6
- hidden: bfloat16 [2048, 28672], P('row', 'col'), may hold values from -0.12988281 to 0.12988281
- weight: bfloat16 [28672, 8192], P('col', 'row'), may hold values from -0.03125 to 0.03125
Outputs:
- token_grad: bfloat16 [2048, 28672], P('row', 'col')
- weight_grad: bfloat16 [28672, 8192], P('col', 'row')
All inputs are finite; a program needn't handle non-finite values.
Results may differ from a plain program's by a relative error of at most 0.001.
Values may be sent and summed in bfloat16 or wider, within the bound.
A program may use at most 64 MiB of HBM per device.

v0:
```python
import jax
import jax.numpy as jnp
from jax import lax
from jax.sharding import PartitionSpec as P


def on_device(out_grad, hidden, weight):
    gathered = lax.all_gather(out_grad, "col", axis=0, tiled=True)
    cotangent = gathered
    weight_sum = lax.dot_general(
        lax.all_gather(hidden, "row", axis=0, tiled=True),
        cotangent,
        (((0,), (0,)), ((), ())),
        preferred_element_type=jnp.float32,
    )
    weight_grad = weight_sum.astype(jnp.bfloat16)
    own_full = lax.all_to_all(gathered, "row", split_axis=0, concat_axis=1, tiled=True)
    cotangent = own_full
    token_sum = lax.dot_general(
        cotangent,
        lax.all_gather(weight, "row", axis=1, tiled=True),
        (((1,), (1,)), ((), ())),
        preferred_element_type=jnp.float32,
    )
    return (token_sum.astype(jnp.bfloat16), weight_grad)


def solution(mesh):
    return jax.shard_map(
        on_device,
        mesh=mesh,
        in_specs=(P("col", "row"), P("row", "col"), P("col", "row")),
        out_specs=(P("row", "col"), P("col", "row")),
        check_vma=False,
    )
```

profile of v0, /device:TPU:1, one launch (start us, length us, event | category | flops | bytes accessed | tf_op | source)
XLA Modules:
  0.0 301.2 jit_solution(12447496459693819890)
XLA Ops:
  7.2 0.0 all-gather.4.cloned.1.call-start
  7.2 0.7 all-gather.4.cloned.1.call-update
  7.9 0.0 all-gather.8.cloned.1.call-start
  7.9 0.7 all-gather.8.cloned.1.call-update
  8.6 0.0 all-gather.6.cloned.1.call-start
  8.7 0.7 all-gather.6.cloned.1.call-update
  9.4 78.3 %all-gather.4.cloned.1.call-done = bf16[2048,512]{1,0:T(8,128)(2,1)} async-done(((bf16[64,512]{1,0:T(8,128)(2,1)}), bf16[2048,512]{1,0:T(8,128)(2,1)}) %all-gather.4.cloned.1.call-update) | async-done | bytes 2097168 | tf_op jit(solution)/shard_map/all_gather | solution.py:8
  87.7 37.9 %all_to_all.19 = bf16[16,128,512]{2,1,0:T(8,128)(2,1)S(1)} all-to-all(bf16[16,128,512]{2,1,0:T(8,128)(2,1)} %bitcast.9), channel_id=1, replica_groups=mesh['row'=16,'col'=32] {'row'}, dimensions={0} | all-to-all | bytes 4194304 | tf_op jit(solution)/shard_map/all_to_all | solution.py:17
  125.6 2.4 copy.5
  127.9 0.0 copy-start
  127.9 28.6 %all-gather.8.cloned.1.call-done = bf16[2048,896]{1,0:T(8,128)(2,1)} async-done(((bf16[128,896]{1,0:T(8,128)(2,1)}), bf16[2048,896]{1,0:T(8,128)(2,1)}) %all-gather.8.cloned.1.call-update) | async-done | bytes 3670032 | tf_op jit(solution)/shard_map/all_gather | solution.py:11
  156.6 5.7 %convolution_convert_fusion = bf16[896,512]{1,0:T(8,128)(2,1)} fusion(bf16[2048,896]{1,0:T(8,128)(2,1)} %all-gather.8.cloned.1.call-done, bf16[2048,512]{1,0:T(8,128)(2,1)} %all-gather.4.cloned.1.call-done), kind=kOutput, calls=%fused_computation | convolution fusion | flops 1879506944 | bytes 6684672 | tf_op jit(solution)/shard_map/dot_general | solution.py:10
  162.3 121.8 %all-gather.6.cloned.1.call-done = bf16[896,8192]{1,0:T(8,128)(2,1)} async-done(((bf16[896,512]{1,0:T(8,128)(2,1)}), bf16[896,8192]{1,0:T(8,128)(2,1)}) %all-gather.6.cloned.1.call-update) | async-done | bytes 14680080 | tf_op jit(solution)/shard_map/all_gather | solution.py:21
  284.1 0.0 copy-done
  284.1 10.6 %convolution_convert_fusion.1 = bf16[128,896]{1,0:T(8,128)(2,1)} fusion(bf16[128,8192]{0,1:T(8,128)(2,1)S(1)} %bitcast.8, bf16[896,8192]{1,0:T(8,128)(2,1)} %all-gather.6.cloned.1.call-done), kind=kOutput, calls=%fused_computation.1 | convolution fusion | flops 1879162880 | bytes 17006592 | tf_op jit(solution)/shard_map/dot_general | solution.py:19
Async XLA Ops:
  7.2 80.5 %all-gather.4.cloned.1.call-start = ((), (), s32[]{:S(2)}) async-start(), calls=%async_computation.1 | async-start | bytes 2162688 | tf_op jit(solution)/shard_map/all_gather | solution.py:8
  7.9 148.7 %all-gather.8.cloned.1.call-start = ((), (), s32[]{:S(2)}) async-start(), calls=%async_computation.3 | async-start | bytes 3899392 | tf_op jit(solution)/shard_map/all_gather | solution.py:11
  8.6 275.4 %all-gather.6.cloned.1.call-start = ((), (), s32[]{:S(2)}) async-start(), calls=%async_computation.2 | async-start | bytes 15597568 | tf_op jit(solution)/shard_map/all_gather | solution.py:21
  127.9 156.1 %copy-start = (bf16[128,16,512]{0,2,1:T(8,128)(2,1)S(1)}, bf16[128,16,512]{0,2,1:T(8,128)(2,1)}, u32[]{:S(2)}) copy-start(bf16[128,16,512]{0,2,1:T(8,128)(2,1)} %copy.5) | copy-start | bytes 6291460
Sparse Core Ops, SparseCore 0:
  10.1 77.5 all-gather.3
  90.7 65.8 all-gather.7
  159.6 124.4 all-gather.5
where the time goes:
time: 301 us
  waiting for transfers between devices  231 us (77%)
  blocking collectives  37.9 us (13%)
  matrix products  16.3 us (5%)
  between operations  13.7 us (5%)
    all_gather x1, waiting for transfers between devices, on_device(): lax.all_gather(weight, 'row', axis=1, tiled=True)  122 us
    all_gather x1, waiting for transfers between devices, on_device(): gathered = lax.all_gather(out_grad, 'col', axis=0, tiled=True)  78.3 us
    all_to_all x1, blocking collectives, on_device(): lax.all_to_all(gathered, 'row', split_axis=0, concat_axis=1, tiled=True)  37.9 us
    all_gather x1, waiting for transfers between devices, on_device(): lax.all_gather(hidden, 'row', axis=0, tiled=True)  28.6 us
    dot_general x1, matrix products, on_device(): lax.dot_general(cotangent, lax.all_gather(weight, 'row', axis=1, tiled=Tr...  10.6 us
  transfers between devices with their start and end apart: 3, of which 3 were waited for; matrix products, arithmetic and copies ran while one was open for 3% of the time, Pallas kernels for 0%

commit v1 on v0

--- a/solution.py
+++ b/solution.py
@@ -4,11 +4,19 @@
 from jax.sharding import PartitionSpec as P
 
 
+def gather_by_exchange(value, axis, dim):
+    size = lax.axis_size(axis)
+    repeats = [size if d == dim else 1 for d in range(value.ndim)]
+    return lax.all_to_all(
+        jnp.tile(value, repeats), axis, split_axis=dim, concat_axis=dim, tiled=True
+    )
+
+
 def on_device(out_grad, hidden, weight):
     gathered = lax.all_gather(out_grad, "col", axis=0, tiled=True)
     cotangent = gathered
     weight_sum = lax.dot_general(
-        lax.all_gather(hidden, "row", axis=0, tiled=True),
+        gather_by_exchange(hidden, "row", 0),
         cotangent,
         (((0,), (0,)), ((), ())),
         preferred_element_type=jnp.float32,

time: 301 us -> 239 us (0.79)
  waiting for transfers between devices: 231 us -> 147 us
  blocking collectives: 37.9 us -> 50.3 us
  starting transfers between devices: 0.11 us -> 6.76 us
    all_gather x1, waiting for transfers between devices: 78.3 us -> 27.1 us  [on_device(): gathered = lax.all_gather(out_grad, 'col', axis=0, tiled=True)]
    all_gather x1, waiting for transfers between devices: 122 us -> 86.1 us  [on_device(): lax.all_gather(weight, 'row', axis=1, tiled=True)]
    all_to_all x0 -> x1, waiting for transfers between devices: none -> 32 us  [on_device(): lax.all_to_all(gathered, 'row', split_axis=0, concat_axis=1, tiled=True)]
    all_gather x1 -> x0, waiting for transfers between devices: 28.6 us -> none  [on_device(): lax.all_gather(hidden, 'row', axis=0, tiled=True)]
    all_to_all x1, blocking collectives: 37.9 us -> 50.3 us  [gather_by_exchange(): lax.all_to_all(jnp.tile(value, repeats), axis, split_axis=dim, concat_axi...]
    all_to_all x0 -> x1, starting transfers between devices: none -> 6.69 us  [on_device(): lax.all_to_all(gathered, 'row', split_axis=0, concat_axis=1, tiled=True)]
  transfers between devices with their start and end apart: 3 -> 3, of which waited for: 3 -> 3; matrix products, arithmetic and copies ran while one was open for 3% -> 4% of each run, Pallas kernels for 0% -> 0%
where the time goes in v1:
time: 239 us; the launch traced here: 238 us
  waiting for transfers between devices  147 us (62%)
  blocking collectives  50.3 us (21%)
  matrix products  16.9 us (7%)
  between operations  14.1 us (6%)
  starting transfers between devices  6.76 us (3%)
  local copies, waits for them, and re-layouts  3.81 us (2%)
    all_gather x1, waiting for transfers between devices, on_device(): lax.all_gather(weight, 'row', axis=1, tiled=True)  86.1 us
    all_to_all x1, blocking collectives, gather_by_exchange(): lax.all_to_all(jnp.tile(value, repeats), axis, split_axis=dim, concat_axi...  50.3 us
    all_to_all x1, waiting for transfers between devices, on_device(): lax.all_to_all(gathered, 'row', split_axis=0, concat_axis=1, tiled=True)  32 us
    all_gather x1, waiting for transfers between devices, on_device(): gathered = lax.all_gather(out_grad, 'col', axis=0, tiled=True)  27.1 us
    dot_general x1, matrix products, on_device(): lax.dot_general(cotangent, lax.all_gather(weight, 'row', axis=1, tiled=Tr...  11.2 us
    all_to_all x1, starting transfers between devices, on_device(): lax.all_to_all(gathered, 'row', split_axis=0, concat_axis=1, tiled=True)  6.69 us
    dot_general x1, matrix products, on_device(): lax.dot_general(gather_by_exchange(hidden, 'row', 0), cotangent, (((0,),...  5.72 us
  transfers between devices with their start and end apart: 3, of which 3 were waited for; matrix products, arithmetic and copies ran while one was open for 4% of the time, Pallas kernels for 0%

profile of v1, /device:TPU:1, one launch (start us, length us, event | category | flops | bytes accessed | tf_op | source)
XLA Modules:
  0.0 238.4 jit_solution(16517772892827461739)
XLA Ops:
  7.2 0.0 all-gather.3.cloned.1.call-start
  7.2 0.7 all-gather.3.cloned.1.call-update
  7.9 0.0 all-gather.5.cloned.1.call-start
  7.9 0.7 all-gather.5.cloned.1.call-update
  8.6 1.4 tile.2
  10.1 50.3 %all_to_all.28 = bf16[16,128,896]{2,1,0:T(8,128)(2,1)} all-to-all(bf16[16,128,896]{2,1,0:T(8,128)(2,1)S(1)} %tile.2), channel_id=1, replica_groups=mesh['row'=16,'col'=32] {'row'}, dimensions={0} | all-to-all | bytes 7340032 | tf_op jit(solution)/shard_map/all_to_all | solution.py:10
  60.4 27.1 %all-gather.3.cloned.1.call-done = bf16[2048,512]{1,0:T(8,128)(2,1)} async-done(((bf16[64,512]{1,0:T(8,128)(2,1)}), bf16[2048,512]{1,0:T(8,128)(2,1)}) %all-gather.3.cloned.1.call-update) | async-done | bytes 2097168 | tf_op jit(solution)/shard_map/all_gather | solution.py:16
  87.4 6.7 %all-to-all-start = ((bf16[16,128,512]{2,1,0:T(8,128)(2,1)}), bf16[16,128,512]{2,1,0:T(8,128)(2,1)S(1)}, u32[]{:S(2)}, u32[]{:S(2)}) async-start(bf16[16,128,512]{2,1,0:T(8,128)(2,1)} %bitcast.11), calls=%async_computation | async-start | bytes 4194304 | tf_op jit(solution)/shard_map/all_to_all | solution.py:25
  94.1 5.7 %convolution_convert_fusion = bf16[896,512]{1,0:T(8,128)(2,1)} fusion(bf16[2048,896]{1,0:T(8,128)(2,1)} %bitcast.10, bf16[2048,512]{1,0:T(8,128)(2,1)} %all-gather.3.cloned.1.call-done), kind=kOutput, calls=%fused_computation | convolution fusion | flops 1879506944 | bytes 6684672 | tf_op jit(solution)/shard_map/dot_general | solution.py:18
  99.9 32.0 %all-to-all-done = bf16[16,128,512]{2,1,0:T(8,128)(2,1)S(1)} async-done(((bf16[16,128,512]{2,1,0:T(8,128)(2,1)}), bf16[16,128,512]{2,1,0:T(8,128)(2,1)S(1)}, u32[]{:S(2)}, u32[]{:S(2)}) %all-to-all-start) | async-done | bytes 2097184 | tf_op jit(solution)/shard_map/all_to_all | solution.py:25
  131.9 2.4 copy.5
  134.2 86.1 %all-gather.5.cloned.1.call-done = bf16[896,8192]{1,0:T(8,128)(2,1)} async-done(((bf16[896,512]{1,0:T(8,128)(2,1)}), bf16[896,8192]{1,0:T(8,128)(2,1)}) %all-gather.5.cloned.1.call-update) | async-done | bytes 14680080 | tf_op jit(solution)/shard_map/all_gather | solution.py:29
  220.3 11.2 %convolution_convert_fusion.1 = bf16[128,896]{1,0:T(8,128)(2,1)} fusion(bf16[128,8192]{0,1:T(8,128)(2,1)} %bitcast.9, bf16[896,8192]{1,0:T(8,128)(2,1)} %all-gather.5.cloned.1.call-done), kind=kOutput, calls=%fused_computation.1 | convolution fusion | flops 1879162880 | bytes 17006592 | tf_op jit(solution)/shard_map/dot_general | solution.py:27
Async XLA Ops:
  7.2 80.3 %all-gather.3.cloned.1.call-start = ((), (), s32[]{:S(2)}) async-start(), calls=%async_computation.2 | async-start | bytes 2162688 | tf_op jit(solution)/shard_map/all_gather | solution.py:16
  7.9 212.4 %all-gather.5.cloned.1.call-start = ((), (), s32[]{:S(2)}) async-start(), calls=%async_computation.3 | async-start | bytes 15597568 | tf_op jit(solution)/shard_map/all_gather | solution.py:29
  87.4 44.4 %all-to-all-start = ((bf16[16,128,512]{2,1,0:T(8,128)(2,1)}), bf16[16,128,512]{2,1,0:T(8,128)(2,1)S(1)}, u32[]{:S(2)}, u32[]{:S(2)}) async-start(bf16[16,128,512]{2,1,0:T(8,128)(2,1)} %bitcast.11), calls=%async_computation | async-start | bytes 4194304 | tf_op jit(solution)/shard_map/all_to_all | solution.py:25
Sparse Core Ops, SparseCore 0:
  10.1 77.2 all-gather.2
  90.4 129.8 all-gather.4
